TPU v7x, 256 devices: a whole 4x4x8 slice. The times are simulated.
256 devices in a mesh: dp: 16 (over z, y_lo), tensor: 4 (over x), section: 4 (over y_hi, core).
Axes of the slice: x: 4, y: 4 (y_hi: 2, y_lo: 2; y = y_hi * 2 + y_lo), z: 8, core: 2. Of those that a mesh axis runs over, the one named last changes fastest.
Arguments:
- grad_parts: bfloat16 [4, 16, 4, 1024, 1024], P('section', 'dp', None, None, 'tensor'), may hold values from -1.5 to 1.5
- first_moment: float32 [4, 4, 1024, 1024], P('section', 'tensor', 'dp'), may hold values from -3 to 3
- second_moment: float32 [4, 4, 1024, 1024], P('section', 'tensor', 'dp'), may hold values from 0.1 to 4
- left_stat: float32 [4, 4, 1024, 1024], P('section', 'tensor', 'dp'), may hold values from -12288 to 184320
- right_stat: float32 [4, 4, 1024, 1024], P('section', 'tensor', 'dp'), may hold values from -12288 to 184320
- left_basis: float32 [4, 4, 1024, 1024], P('section', 'tensor', 'dp'), may hold values from -0.1875 to 0.1875
- right_basis: float32 [4, 4, 1024, 1024], P('section', 'tensor', 'dp'), may hold values from -0.1875 to 0.1875
- gain_grads: float32 [4, 16, 4, 2, 1024], P('section', 'dp', 'tensor'), may hold values from -1.2 to 1.2
- gain_first: float32 [4, 2, 1024], P('section'), may hold values from -3 to 3
- gain_second: float32 [4, 2, 1024], P('section'), may hold values from 0.1 to 4
- table_grads: float32 [4, 16, 32, 16], P('section', 'dp', None, 'tensor'), may hold values from -1.2 to 1.2
- table_first: float32 [32, 16], P(None, 'tensor'), may hold values from -3 to 3
- table_second: float32 [32, 16], P(None, 'tensor'), may hold values from 0.1 to 4
Outputs:
- update: float32 [4, 4, 1024, 1024], P('section', 'tensor', 'dp')
- first_next: float32 [4, 4, 1024, 1024], P('section', 'tensor', 'dp')
- second_next: float32 [4, 4, 1024, 1024], P('section', 'tensor', 'dp')
- left_next: float32 [4, 4, 1024, 1024], P('section', 'tensor', 'dp')
- right_next: float32 [4, 4, 1024, 1024], P('section', 'tensor', 'dp')
- left_rotation: float32 [4, 4, 1024, 1024], P('section', 'tensor', 'dp')
- right_rotation: float32 [4, 4, 1024, 1024], P('section', 'tensor', 'dp')
- gain_update: float32 [4, 2, 1024], P('section')
- gain_moment: float32 [4, 2, 1024], P('section')
- gain_squares: float32 [4, 2, 1024], P('section')
- table_update: float32 [32, 16], P(None, 'tensor')
- table_moment: float32 [32, 16], P(None, 'tensor')
- table_squares: float32 [32, 16], P(None, 'tensor')
All inputs are finite; a program needn't handle non-finite values.
Results may differ from a plain program's by a relative error of at most 0.014.
Values may be sent and summed in bfloat16 or wider, within the bound.
A program may use at most 64 MiB of HBM per device.

v0:
```python
import jax
import jax.numpy as jnp
from jax import lax
from jax.sharding import PartitionSpec as P

NS_ITERS = 3
beta_first = 0.9
beta_second = 0.95
beta_stat = 0.95
adam_eps = 1e-08
norm_eps = 1e-06
step_count = 10.0


def to_half(value):
    return value.astype(jnp.bfloat16)


def batched(pattern, left, right):
    return jnp.einsum(pattern, left, right, preferred_element_type=jnp.float32)


def adam_direction(first, second):
    first_hat = first / (1.0 - beta_first**step_count)
    second_hat = second / (1.0 - beta_second**step_count)
    return first_hat / (jnp.sqrt(second_hat) + adam_eps)


def local(
    grad_parts,
    first_moment,
    second_moment,
    left_stat,
    right_stat,
    left_basis,
    right_basis,
    gain_grads,
    gain_first,
    gain_second,
    table_grads,
    table_first,
    table_second,
):
    partial_value = grad_parts[0, 0]
    columns = lax.all_to_all(partial_value, "tensor", split_axis=0, concat_axis=2, tiled=True)
    summed = lax.psum_scatter(
        columns.astype(jnp.float32).astype(jnp.bfloat16), "dp", scatter_dimension=1, tiled=True
    ).astype(jnp.float32)
    grad_rows = to_half(summed)
    row_count = grad_rows.shape[1]
    offset = lax.axis_index("dp") * row_count
    left_local = to_half(left_basis[0])
    right_local = to_half(right_basis[0])
    left_full, right_full = (
        lax.all_gather(left_local, "dp", axis=1, tiled=True),
        lax.all_gather(right_local, "dp", axis=1, tiled=True),
    )
    grad_full = lax.all_gather(grad_rows, "dp", axis=1, tiled=True)
    rotated_half = to_half(batched("mik,mkj->mij", grad_rows, right_full))
    block = left_local
    rotated = jnp.swapaxes(
        lax.psum_scatter(
            batched("mkc,mkj->cmj", block, rotated_half), "dp", scatter_dimension=0, tiled=True
        ),
        0,
        1,
    )
    first_new = beta_first * first_moment[0] + (1.0 - beta_first) * rotated
    second_new = beta_second * second_moment[0] + (1.0 - beta_second) * rotated * rotated
    direction = to_half(adam_direction(first_new, second_new))
    block = left_local
    back_half = to_half(
        batched("mik,mkj->mij", block, lax.all_gather(direction, "dp", axis=1, tiled=True))
    )
    update = batched("mik,mjk->mij", back_half, right_full)
    grad_columns = lax.dynamic_slice_in_dim(grad_full, offset, row_count, 2)
    left_new = beta_stat * left_stat[0] + batched("mik,mjk->mij", grad_rows, grad_full)
    right_new = beta_stat * right_stat[0] + batched("mki,mkj->mij", grad_columns, grad_full)
    power_left = batched("mik,mkj->mij", to_half(left_new), left_full)
    power_right = batched("mik,mkj->mij", to_half(right_new), right_full)
    power = jnp.concatenate([power_left, power_right], axis=0)
    squares = lax.psum(jnp.sum(power * power, axis=(1, 2)), "dp")
    iterate = power / jnp.sqrt(squares + norm_eps)[:, None, None]
    for sweep in range(NS_ITERS):
        iterate_half = to_half(iterate)
        iterate_full = lax.all_gather(iterate_half, "dp", axis=1, tiled=True)
        gram = to_half(batched("mik,mjk->mij", iterate_half, iterate_full))
        iterate = 1.5 * iterate - 0.5 * batched("mik,mkj->mij", gram, iterate_full)
    local_mats = power_left.shape[0]
    left_rotation = iterate[:local_mats]
    right_rotation = iterate[local_mats:]
    gain_sum = lax.psum(gain_grads[0, 0, 0], ("dp", "tensor"))
    gain_moment = beta_first * gain_first[0] + (1.0 - beta_first) * gain_sum
    gain_squares = beta_second * gain_second[0] + (1.0 - beta_second) * gain_sum * gain_sum
    gain_update = adam_direction(gain_moment, gain_squares)
    table_sum = lax.psum(table_grads[0, 0], ("dp", "section"))
    table_moment = beta_first * table_first + (1.0 - beta_first) * table_sum
    table_squares = beta_second * table_second + (1.0 - beta_second) * table_sum * table_sum
    table_update = adam_direction(table_moment, table_squares)
    return (
        update[None],
        first_new[None],
        second_new[None],
        left_new[None],
        right_new[None],
        left_rotation[None],
        right_rotation[None],
        gain_update[None],
        gain_moment[None],
        gain_squares[None],
        table_update,
        table_moment,
        table_squares,
    )


def solution(mesh):
    return jax.shard_map(
        local,
        mesh=mesh,
        in_specs=(
            P("section", "dp", None, None, "tensor"),
            P("section", "tensor", "dp", None),
            P("section", "tensor", "dp", None),
            P("section", "tensor", "dp", None),
            P("section", "tensor", "dp", None),
            P("section", "tensor", "dp", None),
            P("section", "tensor", "dp", None),
            P("section", "dp", "tensor", None, None),
            P("section", None, None),
            P("section", None, None),
            P("section", "dp", None, "tensor"),
            P(None, "tensor"),
            P(None, "tensor"),
        ),
        out_specs=(
            P("section", "tensor", "dp", None),
            P("section", "tensor", "dp", None),
            P("section", "tensor", "dp", None),
            P("section", "tensor", "dp", None),
            P("section", "tensor", "dp", None),
            P("section", "tensor", "dp", None),
            P("section", "tensor", "dp", None),
            P("section", None, None),
            P("section", None, None),
            P("section", None, None),
            P(None, "tensor"),
            P(None, "tensor"),
            P(None, "tensor"),
        ),
        check_vma=False,
    )
```

profile of v0, /device:TPU:2, one launch (start us, length us, event | category | flops | bytes accessed | tf_op | source)
XLA Modules:
  0.0 1098.2 jit_solution(950655685034763806)
XLA Ops:
  7.2 4.0 copy.47
  11.2 29.7 %all_to_all.18 = bf16[4,1024,256]{1,2,0:T(8,128)(2,1)S(1)} all-to-all(bf16[4,1024,256]{1,2,0:T(8,128)(2,1)} %bitcast.140), channel_id=1, replica_groups=mesh['dp'=16,'tensor'=4,'section'=4] {'tensor'}, dimensions={0} | all-to-all | bytes 4194304 | tf_op jit(solution)/shard_map/all_to_all | solution.py:45
  40.9 7.8 copy.50
  48.7 4.4 copy.60
  53.1 77.8 %reduce-scatter.4.cloned.1.call-done = bf16[64,1024]{1,0:T(8,128)(2,1)} async-done(((bf16[1024,1024]{1,0:T(8,128)(2,1)}), bf16[64,1024]{1,0:T(8,128)(2,1)}) %reduce-scatter.4.cloned.1.call-update) | async-done | bytes 131088
  134.5 70.3 %all-gather.12.cloned.1.call-done = bf16[1,1024,1024]{2,1,0:T(8,128)(2,1)} async-done(((bf16[1,64,1024]{2,1,0:T(8,128)(2,1)}), bf16[1,1024,1024]{2,1,0:T(8,128)(2,1)}) %all-gather.12.cloned.1.call-update) | async-done | bytes 2097168 | tf_op jit(solution)/shard_map/all_gather | solution.py:58
  204.7 2.5 fusion.20
  207.2 70.5 %all-gather.20.cloned.1.call-done = bf16[1,1,1024,1024]{3,2,1,0:T(8,128)(2,1)} async-done(((bf16[1,1,64,1024]{3,2,1,0:T(8,128)(2,1)}), bf16[1,1,1024,1024]{3,2,1,0:T(8,128)(2,1)}) %all-gather.20.cloned.1.call-update) | async-done | bytes 2097168 | tf_op jit(solution)/shard_map/all_gather | solution.py:56
  277.7 2.1 fusion.26
  280.6 69.9 %all-gather.22.cloned.1.call-done = bf16[1,1,1024,1024]{3,2,1,0:T(8,128)(2,1)} async-done(((bf16[1,1,64,1024]{3,2,1,0:T(8,128)(2,1)}), bf16[1,1,1024,1024]{3,2,1,0:T(8,128)(2,1)}) %all-gather.22.cloned.1.call-update) | async-done | bytes 2097168 | tf_op jit(solution)/shard_map/all_gather | solution.py:55
  350.5 2.1 fusion.29
  352.8 32.8 %psum.21 = f32[2]{0:T(128)S(1)} all-reduce(f32[2]{0:T(128)S(1)} %multiply_reduce_fusion), channel_id=1, replica_groups=mesh['dp'=16,'tensor'=4,'section'=4] {'dp'}, use_global_device_ids=true, to_apply=%region_3.0 | all-reduce | flops 2 | bytes 16 | tf_op jit(solution)/shard_map/psum | solution.py:82
  386.5 3.2 convolution_bitcast_fusion
  389.7 11.0 %copy.48 = f32[1024,1,1024]{2,1,0:T(1,128)} copy(f32[1024,1,1024]{0,2,1:T(8,128)} %convolution_bitcast_fusion) | data formatting | bytes 8388608 | tf_op jit(solution)/shard_map/mkc,mkj->cmj/transpose | solution.py:20
  400.9 84.0 %all-gather.14.cloned.1.call-done = bf16[2,1024,1024]{2,1,0:T(8,128)(2,1)} async-done(((bf16[2,64,1024]{2,1,0:T(8,128)(2,1)}), bf16[2,1024,1024]{2,1,0:T(8,128)(2,1)}) %all-gather.14.cloned.1.call-update) | async-done | bytes 4194320 | tf_op jit(solution)/shard_map/all_gather | solution.py:86
  484.9 6.5 fusion.73
  492.7 193.9 %all-reduce.3.cloned.1.call-done = f32[1024,1,1024]{2,1,0:T(1,128)} async-done(((f32[1024,1,1024]{2,1,0:T(1,128)}), f32[1024,1,1024]{2,1,0:T(1,128)}) %all-reduce.3.cloned.1.call-update) | async-done | bytes 4194320
  688.5 99.6 %all-gather.16.cloned.1.call-done = bf16[2,1024,1024]{2,1,0:T(8,128)(2,1)} async-done(((bf16[2,64,1024]{2,1,0:T(8,128)(2,1)}), bf16[2,1024,1024]{2,1,0:T(8,128)(2,1)}) %all-gather.16.cloned.1.call-update) | async-done | bytes 4194320 | tf_op jit(solution)/shard_map/all_gather | solution.py:86
  788.1 6.4 fusion.76
  794.6 128.0 %psum.23 = f32[32,4]{0,1:T(4,128)} all-reduce(f32[32,4]{0,1:T(4,128)S(1)} %bitcast.144), channel_id=1, replica_groups=mesh['dp'=16,'tensor'=4,'section'=4] {'dp','section'}, use_global_device_ids=true, to_apply=%region_5.0 | all-reduce | flops 128 | bytes 1024 | tf_op jit(solution)/shard_map/psum | solution.py:96
  922.6 155.6 %psum.22 = f32[2,1024]{1,0:T(2,128)S(1)} all-reduce(f32[2,1024]{1,0:T(2,128)S(1)} %bitcast.143), channel_id=1, replica_groups=mesh['dp'=16,'tensor'=4,'section'=4] {'dp','tensor'}, use_global_device_ids=true, to_apply=%region_4.0 | all-reduce | flops 2048 | bytes 16384 | tf_op jit(solution)/shard_map/psum | solution.py:92
  1079.5 1.4 fusion.69
  1081.8 3.5 fusion.23
  1085.3 5.6 fusion.14
  (65 shorter events, 11.1 us)
Async XLA Ops:
  7.2 123.7 %reduce-scatter.4.cloned.1.call-start = ((), (), s32[]{:S(2)}) async-start(), calls=%async_computation.9 | async-start | bytes 2228224
  53.0 79.7 %copy-start.8 = (f32[1,1,64,1024]{3,2,1,0:T(8,128)S(1)}, f32[1,1,64,1024]{3,2,1,0:T(8,128)}, u32[]{:S(2)}) copy-start(f32[1,1,64,1024]{3,2,1,0:T(8,128)} %param.19) | copy-start | bytes 786436
  53.0 80.5 %copy-start.9 = (f32[1,1,64,1024]{3,2,1,0:T(8,128)S(1)}, f32[1,1,64,1024]{3,2,1,0:T(8,128)}, u32[]{:S(2)}) copy-start(f32[1,1,64,1024]{3,2,1,0:T(8,128)} %param.18) | copy-start | bytes 786436
  53.0 151.7 %copy-start.10 = (f32[1,1,64,1024]{3,2,1,0:T(8,128)S(1)}, f32[1,1,64,1024]{3,2,1,0:T(8,128)}, u32[]{:S(2)}) copy-start(f32[1,1,64,1024]{3,2,1,0:T(8,128)} %param.17) | copy-start | bytes 786436
  53.1 151.7 %all-gather.12.cloned.1.call-start = ((), (), s32[]{:S(2)}) async-start(), calls=%async_computation.3 | async-start | bytes 2228224 | tf_op jit(solution)/shard_map/all_gather | solution.py:58
  132.7 145.0 %all-gather.20.cloned.1.call-start = ((), (), s32[]{:S(2)}) async-start(), calls=%async_computation.7 | async-start | bytes 2228224 | tf_op jit(solution)/shard_map/all_gather | solution.py:56
  133.5 217.1 %all-gather.22.cloned.1.call-start = ((), (), s32[]{:S(2)}) async-start(), calls=%async_computation.8 | async-start | bytes 2228224 | tf_op jit(solution)/shard_map/all_gather | solution.py:55
  134.2 350.7 %all-gather.14.cloned.1.call-start = ((), (), s32[]{:S(2)}) async-start(), calls=%async_computation.4 | async-start | bytes 4456448 | tf_op jit(solution)/shard_map/all_gather | solution.py:86
  134.5 145.3 %copy-start.11 = (f32[1,1,64,1024]{3,2,1,0:T(8,128)S(1)}, f32[1,1,64,1024]{3,2,1,0:T(8,128)}, u32[]{:S(2)}) copy-start(f32[1,1,64,1024]{3,2,1,0:T(8,128)} %param.16) | copy-start | bytes 786436
  204.7 75.0 %copy-start.1 = (bf16[1,1024,1024]{2,1,0:T(8,128)(2,1)S(1)}, bf16[1,1024,1024]{2,1,0:T(8,128)(2,1)}, u32[]{:S(2)}) copy-start(bf16[1,1024,1024]{2,1,0:T(8,128)(2,1)} %all-gather.12.cloned.1.call-done) | copy-start | bytes 6291460
  207.2 73.4 %copy-start.6 = (f32[64,1024]{1,0:T(8,128)}, f32[64,1024]{1,0:T(8,128)S(1)}, u32[]{:S(2)}) copy-start(f32[64,1024]{1,0:T(8,128)S(1)} %fusion.20) | copy-start | bytes 786436
  280.6 105.9 %copy-start.7 = (f32[64,1024]{1,0:T(8,128)}, f32[64,1024]{1,0:T(8,128)S(1)}, u32[]{:S(2)}) copy-start(f32[64,1024]{1,0:T(8,128)S(1)} %fusion.17) | copy-start | bytes 786436
  280.6 105.9 %copy-start = (bf16[1,1,1024,1024]{3,2,1,0:T(8,128)(2,1)S(1)}, bf16[1,1,1024,1024]{3,2,1,0:T(8,128)(2,1)}, u32[]{:S(2)}) copy-start(bf16[1,1,1024,1024]{3,2,1,0:T(8,128)(2,1)} %all-gather.20.cloned.1.call-done) | copy-start | bytes 6291460
  280.6 105.9 %copy-start.3 = (bf16[1,1,64,1024]{3,2,1,0:T(8,128)(2,1)S(1)}, bf16[1,1,64,1024]{3,2,1,0:T(8,128)(2,1)}, u32[]{:S(2)}) copy-start(bf16[1,1,64,1024]{3,2,1,0:T(8,128)(2,1)} %convert_element_type.87) | copy-start | bytes 393220
  386.4 300.2 %all-reduce.3.cloned.1.call-start = ((), (), s32[]{:S(2)}) async-start(), calls=%async_computation.10 | async-start | bytes 8388608
  400.8 90.7 %copy-start.14 = (u32[256]{0:T(256)S(1)}, u32[256]{0:T(256)}, u32[]{:S(2)}) copy-start(u32[256]{0:T(256)} %constant.66) | copy-start | bytes 3076
  400.8 286.8 %copy-start.4 = (f32[1,1,64,1024]{3,2,1,0:T(8,128)S(1)}, f32[1,1,64,1024]{3,2,1,0:T(8,128)}, u32[]{:S(2)}) copy-start(f32[1,1,64,1024]{3,2,1,0:T(8,128)} %param.15) | copy-start | bytes 786436
  400.8 286.8 %copy-start.5 = (f32[1,1,64,1024]{3,2,1,0:T(8,128)S(1)}, f32[1,1,64,1024]{3,2,1,0:T(8,128)}, u32[]{:S(2)}) copy-start(f32[1,1,64,1024]{3,2,1,0:T(8,128)} %param.14) | copy-start | bytes 786436
  400.8 387.3 %all-gather.16.cloned.1.call-start = ((), (), s32[]{:S(2)}) async-start(), calls=%async_computation.5 | async-start | bytes 4456448 | tf_op jit(solution)/shard_map/all_gather | solution.py:86
  491.4 590.4 %all-gather.10.cloned.1.call-start = ((), (), s32[]{:S(2)}) async-start(), calls=%async_computation.2 | async-start | bytes 2228224 | tf_op jit(solution)/shard_map/all_gather | solution.py:73
  688.5 396.8 %all-gather.18.cloned.1.call-start = ((), (), s32[]{:S(2)}) async-start(), calls=%async_computation.6 | async-start | bytes 4456448 | tf_op jit(solution)/shard_map/all_gather | solution.py:86
  788.1 6.5 copy-start.13
  788.1 134.5 %copy-start.12 = (f32[1,1,1,2,1024]{4,3,2,1,0:T(2,128)S(1)}, f32[1,1,1,2,1024]{4,3,2,1,0:T(2,128)}, u32[]{:S(2)}) copy-start(f32[1,1,1,2,1024]{4,3,2,1,0:T(2,128)} %param.20) | copy-start | bytes 24580
  1081.8 3.5 copy-start.2
Sparse Core Ops, SparseCore 0:
  53.2 77.7 reduce-scatter.3
  133.3 71.4 all-gather.11
  207.1 70.5 all-gather.19
  279.9 70.5 all-gather.21
  386.5 98.3 all-gather.13
  487.4 199.1 all-reduce.2
  689.0 99.1 all-gather.15
  790.5 73.1 all-gather.9
  866.1 98.3 all-gather.17
where the time goes:
time: 1100 us
  waiting for transfers between devices  666 us (61%)
  blocking collectives  346 us (31%)
  matrix products  32.5 us (3%)
  local copies, waits for them, and re-layouts  31.6 us (3%)
  between operations  14.7 us (1%)
    unnamed x11, waiting for transfers between devices  272 us
    all_gather x3, waiting for transfers between devices, local(): iterate_full = lax.all_gather(iterate_half, 'dp', axis=1, tiled=True)  184 us
    psum x1, blocking collectives, local(): gain_sum = lax.psum(gain_grads[0, 0, 0], ('dp', 'tensor'))  156 us
    psum x1, blocking collectives, local(): table_sum = lax.psum(table_grads[0, 0], ('dp', 'section'))  128 us
    all_gather x1, waiting for transfers between devices, local(): lax.all_gather(right_local, 'dp', axis=1, tiled=True)  70.5 us
    all_gather x1, waiting for transfers between devices, local(): grad_full = lax.all_gather(grad_rows, 'dp', axis=1, tiled=True)  70.3 us
    all_gather x1, waiting for transfers between devices, local(): lax.all_gather(left_local, 'dp', axis=1, tiled=True)  69.9 us
    psum x1, blocking collectives, local(): squares = lax.psum(jnp.sum(power * power, axis=(1, 2)), 'dp')  32.8 us
  transfers between devices with their start and end apart: 9, of which 7 were waited for; matrix products, arithmetic and copies ran while one was open for 4% of the time, Pallas kernels for 0%

commit v1 on v0

--- a/solution.py
+++ b/solution.py
@@ -93,7 +93,7 @@
     gain_moment = beta_first * gain_first[0] + (1.0 - beta_first) * gain_sum
     gain_squares = beta_second * gain_second[0] + (1.0 - beta_second) * gain_sum * gain_sum
     gain_update = adam_direction(gain_moment, gain_squares)
-    table_sum = lax.psum(table_grads[0, 0], ("dp", "section"))
+    table_sum = jnp.sum(lax.all_gather(table_grads[0, 0], ("dp", "section")), axis=0)
     table_moment = beta_first * table_first + (1.0 - beta_first) * table_sum
     table_squares = beta_second * table_second + (1.0 - beta_second) * table_sum * table_sum
     table_update = adam_direction(table_moment, table_squares)

time: 1100 us -> 1050 us (0.955)
  blocking collectives: 346 us -> 297 us
    psum x1 -> x0, blocking collectives: 128 us -> none  [local(): table_sum = lax.psum(table_grads[0, 0], ('dp', 'section'))]
    all_gather x0 -> x1, blocking collectives: none -> 77.8 us  [local(): lax.all_gather(table_grads[0, 0], ('dp', 'section'))]
where the time goes in v1:
time: 1050 us
  waiting for transfers between devices  666 us (63%)
  blocking collectives  297 us (28%)
  matrix products  32.5 us (3%)
  local copies, waits for them, and re-layouts  31.6 us (3%)
  between operations  14.7 us (1%)
    unnamed x11, waiting for transfers between devices  272 us
    all_gather x3, waiting for transfers between devices, local(): iterate_full = lax.all_gather(iterate_half, 'dp', axis=1, tiled=True)  184 us
    psum x1, blocking collectives, local(): gain_sum = lax.psum(gain_grads[0, 0, 0], ('dp', 'tensor'))  157 us
    all_gather x1, blocking collectives, local(): lax.all_gather(table_grads[0, 0], ('dp', 'section'))  77.8 us
    all_gather x1, waiting for transfers between devices, local(): lax.all_gather(right_local, 'dp', axis=1, tiled=True)  70.5 us
    all_gather x1, waiting for transfers between devices, local(): grad_full = lax.all_gather(grad_rows, 'dp', axis=1, tiled=True)  70.3 us
    all_gather x1, waiting for transfers between devices, local(): lax.all_gather(left_local, 'dp', axis=1, tiled=True)  69.9 us
    psum x1, blocking collectives, local(): squares = lax.psum(jnp.sum(power * power, axis=(1, 2)), 'dp')  32.8 us
  transfers between devices with their start and end apart: 9, of which 7 were waited for; matrix products, arithmetic and copies ran while one was open for 4% of the time, Pallas kernels for 0%

profile of v1, /device:TPU:2, one launch (start us, length us, event | category | flops | bytes accessed | tf_op | source)
XLA Modules:
  0.0 1050.2 jit_solution(16243675834636730887)
XLA Ops:
  7.2 4.0 copy.47
  11.2 29.7 %all_to_all.18 = bf16[4,1024,256]{1,2,0:T(8,128)(2,1)S(1)} all-to-all(bf16[4,1024,256]{1,2,0:T(8,128)(2,1)} %bitcast.139), channel_id=1, replica_groups=mesh['dp'=16,'tensor'=4,'section'=4] {'tensor'}, dimensions={0} | all-to-all | bytes 4194304 | tf_op jit(solution)/shard_map/all_to_all | solution.py:45
  40.9 7.8 copy.50
  48.7 4.4 copy.60
  53.1 77.8 %reduce-scatter.4.cloned.1.call-done = bf16[64,1024]{1,0:T(8,128)(2,1)} async-done(((bf16[1024,1024]{1,0:T(8,128)(2,1)}), bf16[64,1024]{1,0:T(8,128)(2,1)}) %reduce-scatter.4.cloned.1.call-update) | async-done | bytes 131088
  134.5 70.3 %all-gather.13.cloned.1.call-done = bf16[1,1024,1024]{2,1,0:T(8,128)(2,1)} async-done(((bf16[1,64,1024]{2,1,0:T(8,128)(2,1)}), bf16[1,1024,1024]{2,1,0:T(8,128)(2,1)}) %all-gather.13.cloned.1.call-update) | async-done | bytes 2097168 | tf_op jit(solution)/shard_map/all_gather | solution.py:58
  204.7 2.4 fusion.20
  207.2 70.5 %all-gather.21.cloned.1.call-done = bf16[1,1,1024,1024]{3,2,1,0:T(8,128)(2,1)} async-done(((bf16[1,1,64,1024]{3,2,1,0:T(8,128)(2,1)}), bf16[1,1,1024,1024]{3,2,1,0:T(8,128)(2,1)}) %all-gather.21.cloned.1.call-update) | async-done | bytes 2097168 | tf_op jit(solution)/shard_map/all_gather | solution.py:56
  277.7 2.1 fusion.26
  280.6 69.9 %all-gather.23.cloned.1.call-done = bf16[1,1,1024,1024]{3,2,1,0:T(8,128)(2,1)} async-done(((bf16[1,1,64,1024]{3,2,1,0:T(8,128)(2,1)}), bf16[1,1,1024,1024]{3,2,1,0:T(8,128)(2,1)}) %all-gather.23.cloned.1.call-update) | async-done | bytes 2097168 | tf_op jit(solution)/shard_map/all_gather | solution.py:55
  350.5 2.1 fusion.29
  352.8 32.8 %psum.14 = f32[2]{0:T(128)S(1)} all-reduce(f32[2]{0:T(128)S(1)} %multiply_reduce_fusion), channel_id=1, replica_groups=mesh['dp'=16,'tensor'=4,'section'=4] {'dp'}, use_global_device_ids=true, to_apply=%region_3.0 | all-reduce | flops 2 | bytes 16 | tf_op jit(solution)/shard_map/psum | solution.py:82
  386.5 3.2 convolution_bitcast_fusion
  389.7 11.0 %copy.48 = f32[1024,1,1024]{2,1,0:T(1,128)} copy(f32[1024,1,1024]{0,2,1:T(8,128)} %convolution_bitcast_fusion) | data formatting | bytes 8388608 | tf_op jit(solution)/shard_map/mkc,mkj->cmj/transpose | solution.py:20
  400.9 84.0 %all-gather.15.cloned.1.call-done = bf16[2,1024,1024]{2,1,0:T(8,128)(2,1)} async-done(((bf16[2,64,1024]{2,1,0:T(8,128)(2,1)}), bf16[2,1024,1024]{2,1,0:T(8,128)(2,1)}) %all-gather.15.cloned.1.call-update) | async-done | bytes 4194320 | tf_op jit(solution)/shard_map/all_gather | solution.py:86
  484.9 6.5 fusion.73
  492.7 193.9 %all-reduce.3.cloned.1.call-done = f32[1024,1,1024]{2,1,0:T(1,128)} async-done(((f32[1024,1,1024]{2,1,0:T(1,128)}), f32[1024,1,1024]{2,1,0:T(1,128)}) %all-reduce.3.cloned.1.call-update) | async-done | bytes 4194320
  688.5 99.6 %all-gather.17.cloned.1.call-done = bf16[2,1024,1024]{2,1,0:T(8,128)(2,1)} async-done(((bf16[2,64,1024]{2,1,0:T(8,128)(2,1)}), bf16[2,1024,1024]{2,1,0:T(8,128)(2,1)}) %all-gather.17.cloned.1.call-update) | async-done | bytes 4194320 | tf_op jit(solution)/shard_map/all_gather | solution.py:86
  788.1 6.5 fusion.76
  794.6 77.8 %all-gather.2 = f32[64,1,32,4]{2,3,1,0:T(4,128)} all-gather(f32[1,1,32,4]{2,3,1,0:T(4,128)S(1)} %copy-done.12), channel_id=4, replica_groups=mesh['dp'=16,'tensor'=4,'section'=4] {'dp','section'}, dimensions={0}, use_global_device_ids=true | all-gather | bytes 33280 | tf_op jit(solution)/shard_map/all_gather | solution.py:96
  873.3 156.9 %psum.15 = f32[2,1024]{1,0:T(2,128)S(1)} all-reduce(f32[2,1024]{1,0:T(2,128)} %bitcast.142), channel_id=1, replica_groups=mesh['dp'=16,'tensor'=4,'section'=4] {'dp','tensor'}, use_global_device_ids=true, to_apply=%region_4.0 | all-reduce | flops 2048 | bytes 16384 | tf_op jit(solution)/shard_map/psum | solution.py:92
  1031.5 1.4 fusion.69
  1033.8 3.5 fusion.23
  1037.3 5.6 fusion.14
  (66 shorter events, 12.1 us)
Async XLA Ops:
  7.2 123.7 %reduce-scatter.4.cloned.1.call-start = ((), (), s32[]{:S(2)}) async-start(), calls=%async_computation.9 | async-start | bytes 2228224
  53.0 79.7 %copy-start.8 = (f32[1,1,64,1024]{3,2,1,0:T(8,128)S(1)}, f32[1,1,64,1024]{3,2,1,0:T(8,128)}, u32[]{:S(2)}) copy-start(f32[1,1,64,1024]{3,2,1,0:T(8,128)} %param.19) | copy-start | bytes 786436
  53.0 80.5 %copy-start.9 = (f32[1,1,64,1024]{3,2,1,0:T(8,128)S(1)}, f32[1,1,64,1024]{3,2,1,0:T(8,128)}, u32[]{:S(2)}) copy-start(f32[1,1,64,1024]{3,2,1,0:T(8,128)} %param.18) | copy-start | bytes 786436
  53.0 151.7 %copy-start.10 = (f32[1,1,64,1024]{3,2,1,0:T(8,128)S(1)}, f32[1,1,64,1024]{3,2,1,0:T(8,128)}, u32[]{:S(2)}) copy-start(f32[1,1,64,1024]{3,2,1,0:T(8,128)} %param.17) | copy-start | bytes 786436
  53.1 151.7 %all-gather.13.cloned.1.call-start = ((), (), s32[]{:S(2)}) async-start(), calls=%async_computation.3 | async-start | bytes 2228224 | tf_op jit(solution)/shard_map/all_gather | solution.py:58
  132.7 145.0 %all-gather.21.cloned.1.call-start = ((), (), s32[]{:S(2)}) async-start(), calls=%async_computation.7 | async-start | bytes 2228224 | tf_op jit(solution)/shard_map/all_gather | solution.py:56
  133.5 217.1 %all-gather.23.cloned.1.call-start = ((), (), s32[]{:S(2)}) async-start(), calls=%async_computation.8 | async-start | bytes 2228224 | tf_op jit(solution)/shard_map/all_gather | solution.py:55
  134.2 350.7 %all-gather.15.cloned.1.call-start = ((), (), s32[]{:S(2)}) async-start(), calls=%async_computation.4 | async-start | bytes 4456448 | tf_op jit(solution)/shard_map/all_gather | solution.py:86
  134.5 145.3 %copy-start.11 = (f32[1,1,64,1024]{3,2,1,0:T(8,128)S(1)}, f32[1,1,64,1024]{3,2,1,0:T(8,128)}, u32[]{:S(2)}) copy-start(f32[1,1,64,1024]{3,2,1,0:T(8,128)} %param.16) | copy-start | bytes 786436
  204.7 75.0 %copy-start.1 = (bf16[1,1024,1024]{2,1,0:T(8,128)(2,1)S(1)}, bf16[1,1024,1024]{2,1,0:T(8,128)(2,1)}, u32[]{:S(2)}) copy-start(bf16[1,1024,1024]{2,1,0:T(8,128)(2,1)} %all-gather.13.cloned.1.call-done) | copy-start | bytes 6291460
  207.2 73.4 %copy-start.6 = (f32[64,1024]{1,0:T(8,128)}, f32[64,1024]{1,0:T(8,128)S(1)}, u32[]{:S(2)}) copy-start(f32[64,1024]{1,0:T(8,128)S(1)} %fusion.20) | copy-start | bytes 786436
  280.6 105.9 %copy-start.7 = (f32[64,1024]{1,0:T(8,128)}, f32[64,1024]{1,0:T(8,128)S(1)}, u32[]{:S(2)}) copy-start(f32[64,1024]{1,0:T(8,128)S(1)} %fusion.17) | copy-start | bytes 786436
  280.6 105.9 %copy-start = (bf16[1,1,1024,1024]{3,2,1,0:T(8,128)(2,1)S(1)}, bf16[1,1,1024,1024]{3,2,1,0:T(8,128)(2,1)}, u32[]{:S(2)}) copy-start(bf16[1,1,1024,1024]{3,2,1,0:T(8,128)(2,1)} %all-gather.21.cloned.1.call-done) | copy-start | bytes 6291460
  280.6 105.9 %copy-start.3 = (bf16[1,1,64,1024]{3,2,1,0:T(8,128)(2,1)S(1)}, bf16[1,1,64,1024]{3,2,1,0:T(8,128)(2,1)}, u32[]{:S(2)}) copy-start(bf16[1,1,64,1024]{3,2,1,0:T(8,128)(2,1)} %convert_element_type.87) | copy-start | bytes 393220
  386.4 300.2 %all-reduce.3.cloned.1.call-start = ((), (), s32[]{:S(2)}) async-start(), calls=%async_computation.10 | async-start | bytes 8388608
  400.8 90.7 %copy-start.14 = (u32[256]{0:T(256)S(1)}, u32[256]{0:T(256)}, u32[]{:S(2)}) copy-start(u32[256]{0:T(256)} %constant.66) | copy-start | bytes 3076
  400.8 286.8 %copy-start.4 = (f32[1,1,64,1024]{3,2,1,0:T(8,128)S(1)}, f32[1,1,64,1024]{3,2,1,0:T(8,128)}, u32[]{:S(2)}) copy-start(f32[1,1,64,1024]{3,2,1,0:T(8,128)} %param.15) | copy-start | bytes 786436
  400.8 286.8 %copy-start.5 = (f32[1,1,64,1024]{3,2,1,0:T(8,128)S(1)}, f32[1,1,64,1024]{3,2,1,0:T(8,128)}, u32[]{:S(2)}) copy-start(f32[1,1,64,1024]{3,2,1,0:T(8,128)} %param.14) | copy-start | bytes 786436
  400.8 387.3 %all-gather.17.cloned.1.call-start = ((), (), s32[]{:S(2)}) async-start(), calls=%async_computation.5 | async-start | bytes 4456448 | tf_op jit(solution)/shard_map/all_gather | solution.py:86
  491.4 542.4 %all-gather.11.cloned.1.call-start = ((), (), s32[]{:S(2)}) async-start(), calls=%async_computation.2 | async-start | bytes 2228224 | tf_op jit(solution)/shard_map/all_gather | solution.py:73
  688.4 348.8 %all-gather.19.cloned.1.call-start = ((), (), s32[]{:S(2)}) async-start(), calls=%async_computation.6 | async-start | bytes 4456448 | tf_op jit(solution)/shard_map/all_gather | solution.py:86
  788.1 6.5 copy-start.12
  788.1 242.1 %copy-start.13 = (f32[32,4]{0,1:T(4,128)S(1)}, f32[32,4]{0,1:T(4,128)}, u32[]{:S(2)}) copy-start(f32[32,4]{0,1:T(4,128)} %param.24) | copy-start | bytes 1540
  1033.8 3.5 copy-start.2
Sparse Core Ops, SparseCore 0:
  53.2 77.7 reduce-scatter.3
  133.3 71.4 all-gather.12
  207.1 70.5 all-gather.20
  279.9 70.5 all-gather.22
  386.5 98.2 all-gather.14
  487.4 199.1 all-reduce.2
  689.0 99.1 all-gather.16
  790.5 72.3 all-gather.10
  865.2 97.3 all-gather.18
